TPU v7x, 128 devices: a whole 4x4x4 slice. The times are simulated.
128 devices in a mesh: sky: 16 (over x, z), depth: 8 (over y, core).
Axes of the slice: x: 4, y: 4, z: 4, core: 2. Of those that a mesh axis runs over, the one named last changes fastest.
Arguments:
- positions: float32 [3, 2048, 128], P(None, ('sky', 'depth')), may hold values from 0 to 1
- cell_points: int32 [2048], P(('sky', 'depth')), may hold values from 1 to 128
- target_log: float32 [16], replicated, may hold values from 8 to 20
- export_count: int32 [128, 128], P(('sky', 'depth')), may hold values from 0 to 3, as said below
- export_cell: int32 [128, 128, 3], P(('sky', 'depth')), may hold values from 0 to 15
- import_pair: int32 [128, 128, 3], P(('sky', 'depth')), may hold values from 0 to 15
- import_shift: int32 [3, 128, 128, 3], P(None, ('sky', 'depth')), may hold values from -1 to 1, as said below
Outputs:
- travel: float32 [3, 2048, 128], P(None, ('sky', 'depth'))
Inputs may be any that keep to these rules, and one draw needn't show every extreme that they name: export_count[s, t] counts the slots of export_cell[s, t] that are used; it is zero unless s and t are distinct devices whose sky indices differ by at most one modulo the sky axis's size and whose depth indices differ by at most one; in every draw some device t receives 3 cells from each such neighbour. For neighbouring devices t and s, components 0 and 2 of import_shift[:, t, s, k] are the sky step and the depth step from t's region to s's region (sky taken around the cycle), component 1 varies; all components are zero for devices that are not neighbours.
All inputs are finite; a program needn't handle non-finite values.
Results may differ from a plain program's by a relative error of at most 0.00022.
Values sent between devices are 32-bit elements; how exact they have to be, the bound alone decides.
No kernel may reach another device: no remote copies, remote signals or barrier semaphores. Data moves between devices by JAX's collectives and lax.ppermute only.
A program may use at most 64 MiB of HBM per device.

v0:
```python
import jax
import jax.numpy as jnp
from jax import lax
from jax.sharding import PartitionSpec as P

STEPS = 2
EPS_SQ = 0.0001
INV_WIDTH = 16.0
STEP_SIZE = 0.01
ROW_BLOCK = 8


def from_behind(array, axis, by):
    size = lax.axis_size(axis)
    return lax.ppermute(array, axis, [(i, (i + by) % size) for i in range(size)])


def from_behind_2(value, axis, steps):
    count = lax.axis_size(axis)
    initial, last = (max(0, -steps), min(count, count - steps))
    return lax.ppermute(value, axis, [(source, source + steps) for source in range(initial, last)])


def pair_geometry(left_pos, left_mask, right_pos, right_mask, shifts, centres):
    offsets = left_pos[:, :, :, None] - right_pos[:, :, None, :] - shifts[:, :, None, None]
    radius = jnp.sqrt(jnp.sum(offsets * offsets, axis=0) + EPS_SQ)
    weight = left_mask[:, :, None] * right_mask[:, None, :]
    scaled = (radius[None] - centres[:, None, None, None]) * INV_WIDTH
    kernel = jnp.exp(-0.5 * scaled * scaled)
    return (offsets, radius, weight, scaled, kernel)


def block_counts(left_pos, left_mask, right_pos, right_mask, shifts, centres):
    offsets, radius, weight, scaled, kernel = pair_geometry(
        left_pos, left_mask, right_pos, right_mask, shifts, centres
    )
    return jnp.sum(weight[None] * kernel, axis=(1, 2, 3))


def block_forces(left_pos, left_mask, right_pos, right_mask, shifts, centres, bin_pull):
    offsets, radius, weight, scaled, kernel = pair_geometry(
        left_pos, left_mask, right_pos, right_mask, shifts, centres
    )
    slopes = jnp.sum(bin_pull[:, None, None, None] * scaled * kernel, axis=0) * -INV_WIDTH
    strength = weight * slopes / radius
    pulled = strength[None] * offsets
    return (jnp.sum(pulled, axis=3), -jnp.sum(pulled, axis=2))


def take_block(left_pos, left_mask, right_pos, right_mask, shifts, first_row):
    return (
        lax.dynamic_slice_in_dim(left_pos, first_row, ROW_BLOCK, 1),
        lax.dynamic_slice_in_dim(left_mask, first_row, ROW_BLOCK, 0),
        lax.dynamic_slice_in_dim(right_pos, first_row, ROW_BLOCK, 1),
        lax.dynamic_slice_in_dim(right_mask, first_row, ROW_BLOCK, 0),
        lax.dynamic_slice_in_dim(shifts, first_row, ROW_BLOCK, 1),
    )


def ghost_counts(left_pos, left_mask, right_pos, right_mask, shifts, centres):
    block_total = left_pos.shape[1] // ROW_BLOCK

    def add_block(block_id, running):
        pieces = take_block(
            left_pos, left_mask, right_pos, right_mask, shifts, block_id * ROW_BLOCK
        )
        return running + block_counts(
            pieces[0], pieces[1], pieces[2], pieces[3], pieces[4], centres
        )

    return lax.fori_loop(0, block_total, add_block, jnp.zeros(centres.shape, jnp.float32))


def ghost_forces(left_pos, left_mask, right_pos, right_mask, shifts, centres, bin_pull):
    block_total = left_pos.shape[1] // ROW_BLOCK

    def add_block(block_id, buffers):
        first_row = block_id * ROW_BLOCK
        pieces = take_block(left_pos, left_mask, right_pos, right_mask, shifts, first_row)
        force_left, force_right = block_forces(
            pieces[0], pieces[1], pieces[2], pieces[3], pieces[4], centres, bin_pull
        )
        return (
            lax.dynamic_update_slice_in_dim(buffers[0], force_left, first_row, 1),
            lax.dynamic_update_slice_in_dim(buffers[1], force_right, first_row, 1),
        )

    empty = jnp.zeros(left_pos.shape, jnp.float32)
    return lax.fori_loop(0, block_total, add_block, (empty, empty))


def region_offsets():
    return [
        (across, along)
        for across in (-1, 0, 1)
        for along in (-1, 0, 1)
        if (across, along) != (0, 0)
    ]


def neighbour_table():
    sky_here = lax.axis_index("sky")
    depth_here = lax.axis_index("depth")
    sky_count = lax.axis_size("sky")
    depth_count = lax.axis_size("depth")
    near_ids = []
    near_valid = []
    for across, along in region_offsets():
        depth_there = depth_here + along
        inside = (depth_there >= 0) & (depth_there < depth_count)
        clamped = jnp.clip(depth_there, 0, depth_count - 1)
        near_ids.append((sky_here + across) % sky_count * depth_count + clamped)
        near_valid.append(inside)
    return (jnp.stack(near_ids), jnp.stack(near_valid))


def near_sizes(sizes_near):
    received = [None] * 8
    for index, (across, along) in enumerate(region_offsets()):
        piece = sizes_near[index]
        if across != 0:
            piece = from_behind(piece, "sky", across)
        if along != 0:
            piece = from_behind_2(piece, "depth", along)
        received[7 - index] = piece
    return jnp.stack(received)


def near_cells(cells_near):
    received = [None] * 8
    for index, (across, along) in enumerate(region_offsets()):
        piece = cells_near[:, index]
        if across != 0:
            piece = from_behind(piece, "sky", across)
        if along != 0:
            piece = from_behind_2(piece, "depth", along)
        received[7 - index] = piece
    return jnp.stack(received, axis=1)


def near_forces(forces_near):
    received = [None] * 8
    for index, (across, along) in enumerate(region_offsets()):
        piece = forces_near[:, index]
        if across != 0:
            piece = from_behind(piece, "sky", across)
        if along != 0:
            piece = from_behind_2(piece, "depth", along)
        received[7 - index] = piece
    return jnp.stack(received, axis=1)


def send_sizes(sizes_out, near_ids, near_valid):
    return near_sizes(sizes_out[near_ids] * near_valid[:, None].astype(jnp.int32))


def send_cells(coords, export_row, near_ids):
    peer_count, slot_count = export_row.shape
    outgoing = coords[:, export_row[near_ids].reshape(-1)].reshape(
        3, 8, slot_count, coords.shape[2]
    )
    return near_cells(outgoing)


def send_forces(forces_near):
    return near_forces(forces_near)


def body(positions, cell_points, target_log, export_count, export_cell, import_pair, import_shift):
    cell_count = positions.shape[1]
    points = positions.shape[2]
    slot_count = export_cell.shape[2]
    ghosts = 8 * slot_count
    centres = (jnp.arange(target_log.shape[0], dtype=jnp.float32) + 0.5) / INV_WIDTH
    point_ids = jnp.arange(points, dtype=jnp.int32)
    point_mask = (point_ids[None, :] < cell_points[:, None]).astype(jnp.float32)
    cell_ids = jnp.arange(cell_count, dtype=jnp.int32)
    near_ids, near_valid = neighbour_table()
    live_out = jnp.arange(slot_count, dtype=jnp.int32)[None, :] < export_count[0][:, None]
    sizes_out = jnp.where(live_out, cell_points[export_cell[0]], 0)
    sizes_in = send_sizes(sizes_out, near_ids, near_valid)
    ghost_mask = (point_ids[None, :] < sizes_in.reshape(-1)[:, None]).astype(jnp.float32)
    cells_near = export_cell[0][near_ids].reshape(-1)
    live_near = (live_out[near_ids] & near_valid[:, None]).reshape(-1)
    pair_cells = import_pair[0][near_ids].reshape(-1)
    shifts = import_shift[:, 0][:, near_ids].reshape(3, ghosts).astype(jnp.float32)
    left_mask = point_mask[pair_cells]
    onehot_pair = (pair_cells[:, None] == cell_ids[None, :]).astype(jnp.float32)
    onehot_out = ((cells_near[:, None] == cell_ids[None, :]) & live_near[:, None]).astype(
        jnp.float32
    )
    zero_shift = jnp.zeros((3, cell_count), jnp.float32)
    valid_local = jnp.sum(point_mask)
    coords = positions
    travel = jnp.zeros_like(positions)
    for iteration in range(STEPS):
        ghost_pos = send_cells(coords, export_cell[0], near_ids).reshape(3, ghosts, points)
        left_pos = coords[:, pair_cells]
        self_total = block_counts(coords, point_mask, coords, point_mask, zero_shift, centres)
        ghost_total = ghost_counts(left_pos, left_mask, ghost_pos, ghost_mask, shifts, centres)
        counts = lax.psum(0.5 * self_total + ghost_total, ("sky", "depth"))
        mean_count = jnp.mean(counts)
        bin_pull = (jnp.log(1.0 + counts) - target_log) * mean_count / (1.0 + counts)
        self_grad, unused_right = block_forces(
            coords, point_mask, coords, point_mask, zero_shift, centres, bin_pull
        )
        force_left, force_right = ghost_forces(
            left_pos, left_mask, ghost_pos, ghost_mask, shifts, centres, bin_pull
        )
        returned = send_forces(force_right.reshape(3, 8, slot_count, points)).reshape(
            3, ghosts, points
        )
        gradient = self_grad
        gradient = gradient + jnp.einsum(
            "gc,kgp->kcp", onehot_pair, force_left, precision=lax.Precision.HIGHEST
        )
        gradient = gradient + jnp.einsum(
            "gc,kgp->kcp", onehot_out, returned, precision=lax.Precision.HIGHEST
        )
        power_sum, valid_count = lax.psum(
            (jnp.sum(gradient * gradient), valid_local), ("sky", "depth")
        )
        grad_rms = jnp.sqrt(power_sum / (3.0 * valid_count) + 1e-06)
        move_dir = -gradient / grad_rms
        travel = travel + move_dir
        coords = coords + STEP_SIZE * move_dir
    return travel


def solution(mesh):
    in_specs = (
        P(None, ("sky", "depth"), None),
        P(("sky", "depth")),
        P(),
        P(("sky", "depth"), None),
        P(("sky", "depth"), None, None),
        P(("sky", "depth"), None, None),
        P(None, ("sky", "depth"), None, None),
    )
    out_specs = P(None, ("sky", "depth"), None)
    return jax.shard_map(body, mesh=mesh, in_specs=in_specs, out_specs=out_specs, check_vma=False)
```

profile of v0, /device:TPU:1, one launch (start us, length us, event | category | flops | bytes accessed | tf_op | source)
XLA Modules:
  0.0 525.2 jit_solution(16160007866016866266)
XLA Ops:
  3.0 10.6 %fusion.60 = s32[128,3]{1,0:T(8,128)S(1)} fusion(s32[1,128,3]{2,1,0:T(8,128)S(1)} %copy.87, s32[]{:T(128)} %bitcast.31, s32[]{:T(128)} %bitcast.32, s32[]{:T(128)} %bitcast.33, s32[]{:T(128)} %bitcast.34, s32[]{:T(128)} %bitcast.35, s32[]{:T(128)} %bitcast.37, s32[]{:T(128)} %bitcast.36, s32[]{:T(128)} %bitcast.14, s32[]{:T(128)} %bitcast.16, s32[]{:T(128)} %bitcast.18, ...), kind=kLoop, calls=%fused_computation.175 | loop fusion | flops 13440 | bytes 3648 | tf_op jit(solution)/shard_map/jit(_where)/select_n | solution.py:180
  19.7 4.6 collective-permute-start.5
  31.1 5.1 fusion.36
  39.6 4.8 collective-permute-start.7
  47.4 5.0 collective-permute-start.17
  57.6 2.9 collective-permute-done.4
  65.6 2.9 collective-permute-done.11
  70.5 3.6 collective-permute-start.13
  74.9 3.4 collective-permute-start.19
  81.1 3.0 collective-permute-start.21
  84.2 5.6 %collective-permute-start.20 = (f32[3,3,128]{2,1,0:T(4,128)S(1)}, f32[3,3,128]{2,1,0:T(4,128)S(1)}, u32[]{:S(2)}, u32[]{:S(2)}) collective-permute-start(f32[3,3,128]{2,1,0:T(4,128)S(1)} %collective-permute-done.19), channel_id=1, source_target_pairs={{0,1},{1,2},{2,3},{3,4},{4,5},{5,6},{6,7},{8,9},{9,10},{10,11},{11... | collective-permute-start | bytes 13832 | tf_op jit(solution)/shard_map/ppermute | solution.py:21
  91.8 2.9 collective-permute-done.23
  94.8 10.7 %while.70 = (s32[]{:T(128)}, f32[16]{0:T(128)S(1)}, f32[24,128]{1,0:T(8,128)S(1)}, f32[24,128]{1,0:T(8,128)S(1)}, f32[3,24,128]{2,1,0:T(8,128)S(1)}, /*index=5*/...) while((s32[]{:T(128)}, f32[16]{0:T(128)S(1)}, ...), condition=%wide.region_5.6_spmd.clone, body=%wide.region_2.5_spmd.clone.sunk | while | flops 14286903 | bytes 3244889 | solution.py:71
  95.8 2.5 fusion.98
  99.3 2.5 fusion.98
  105.6 62.9 %psum.38 = f32[16]{0:T(128)S(1)} all-reduce(f32[16]{0:T(128)S(1)} %multiply_add_fusion.2), channel_id=1, replica_groups=mesh['sky'=16,'depth'=8] {'sky','depth'}, use_global_device_ids=true, to_apply=%region_6.7 | all-reduce | flops 16 | bytes 128 | tf_op jit(solution)/shard_map/psum | solution.py:201
  169.6 5.4 %fusion.37 = f32[16,128,128]{2,1,0:T(8,128)S(1)} fusion(f32[16]{0:T(128)S(1)} %get-tuple-element.1089, f32[16]{0:T(128)S(1)} %add_multiply_fusion.4, f32[16,128,128]{2,1,0:T(8,128)S(1)} %get-tuple-element.1163), kind=kLoop, calls=%fused_computation.105 | loop fusion | flops 29097984 | bytes 2097280 | tf_op jit(solution)/shard_map/reduce_sum | solution.py:44
  175.4 14.3 %while.68 = (s32[]{:T(128)}, f32[3,24,128]{2,1,0:T(8,128)S(1)}, f32[3,24,128]{2,1,0:T(8,128)S(1)}, f32[24,128]{1,0:T(8,128)S(1)}, f32[24,128]{1,0:T(8,128)S(1)},...) while((s32[]{:T(128)}, f32[3,24,128]{2,1,0:T(8,128)S(1)}, ...), condition=%wide.region_15.16_spmd.clone, body=%wide.region_10.0_spmd.clone.sunk | while | flops 18740276 | bytes 4916107 | solution.py:89
  176.2 2.7 fusion.94
  180.9 2.7 fusion.94
  185.7 2.7 fusion.94
  194.3 3.1 collective-permute-start.29
  199.4 3.6 collective-permute-start.25
  203.8 4.1 collective-permute-start.31
  210.2 3.7 collective-permute-start.33
  213.9 5.3 %collective-permute-start.32 = (f32[3,3,128]{2,1,0:T(4,128)S(1)}, f32[3,3,128]{2,1,0:T(4,128)S(1)}, u32[]{:S(2)}, u32[]{:S(2)}) collective-permute-start(f32[3,3,128]{2,1,0:T(4,128)S(1)} %collective-permute-done.31), channel_id=1, source_target_pairs={{0,1},{1,2},{2,3},{3,4},{4,5},{5,6},{6,7},{8,9},{9,10},{10,11},{11... | collective-permute-start | bytes 13832 | tf_op jit(solution)/shard_map/ppermute | solution.py:21
  221.3 2.9 collective-permute-done.35
  225.0 62.3 %all-reduce = (f32[]{:T(128)}, f32[]{:T(128)}) all-reduce(f32[]{:T(128)} %get-tuple-element.1159, f32[]{:T(128)} %fusion.76), channel_id=1, replica_groups=mesh['sky'=16,'depth'=8] {'sky','depth'}, use_global_device_ids=true, to_apply=%region_17.18 | all-reduce | flops 2 | bytes 16 | tf_op jit(solution)/shard_map/psum | solution.py:220
  291.5 4.8 collective-permute-done.36
  296.3 4.4 collective-permute-start.37
  300.8 5.1 fusion.42
  311.0 4.8 collective-permute-start.43
  321.8 4.7 collective-permute-start.44
  328.6 2.9 collective-permute-done.47
  331.5 10.7 %while.71 = (s32[]{:T(128)}, f32[16]{0:T(128)S(1)}, f32[24,128]{1,0:T(8,128)S(1)}, f32[24,128]{1,0:T(8,128)S(1)}, f32[3,24,128]{2,1,0:T(8,128)S(1)}, /*index=5*/...) while((s32[]{:T(128)}, f32[16]{0:T(128)S(1)}, ...), condition=%wide.region_25.26_spmd.clone, body=%wide.region_22.25_spmd.clone.sunk | while | flops 14286903 | bytes 3244889 | solution.py:71
  342.2 62.2 %psum.41 = f32[16]{0:T(128)S(1)} all-reduce(f32[16]{0:T(128)S(1)} %multiply_add_fusion.1), channel_id=1, replica_groups=mesh['sky'=16,'depth'=8] {'sky','depth'}, use_global_device_ids=true, to_apply=%region_26.27 | all-reduce | flops 16 | bytes 128 | tf_op jit(solution)/shard_map/psum | solution.py:201
  405.7 5.4 %fusion.43 = f32[16,128,128]{2,1,0:T(8,128)S(1)} fusion(f32[16]{0:T(128)S(1)} %get-tuple-element.1087, f32[16,128,128]{2,1,0:T(8,128)S(1)} %add_sqrt_fusion.4, f32[16]{0:T(128)S(1)} %add_multiply_fusion.4), kind=kLoop, calls=%fused_computation.111 | loop fusion | flops 29097984 | bytes 2097280 | tf_op jit(solution)/shard_map/reduce_sum | solution.py:44
  411.5 14.3 %while.69 = (s32[]{:T(128)}, f32[3,24,128]{2,1,0:T(8,128)S(1)}, f32[3,24,128]{2,1,0:T(8,128)S(1)}, f32[24,128]{1,0:T(8,128)S(1)}, f32[24,128]{1,0:T(8,128)S(1)},...) while((s32[]{:T(128)}, f32[3,24,128]{2,1,0:T(8,128)S(1)}, ...), condition=%wide.region_35.36_spmd.clone, body=%wide.region_30.0_spmd.clone.sunk | while | flops 18740276 | bytes 4916107 | solution.py:89
  412.3 2.7 fusion.96
  417.0 2.7 fusion.96
  421.8 2.7 fusion.96
  430.7 3.3 collective-permute-start.53
  435.9 3.6 collective-permute-start.49
  440.3 3.8 collective-permute-start.55
  446.6 3.7 collective-permute-start.57
  450.2 5.3 %collective-permute-start.56 = (f32[3,3,128]{2,1,0:T(4,128)S(1)}, f32[3,3,128]{2,1,0:T(4,128)S(1)}, u32[]{:S(2)}, u32[]{:S(2)}) collective-permute-start(f32[3,3,128]{2,1,0:T(4,128)S(1)} %collective-permute-done.55), channel_id=1, source_target_pairs={{0,1},{1,2},{2,3},{3,4},{4,5},{5,6},{6,7},{8,9},{9,10},{10,11},{11... | collective-permute-start | bytes 13832 | tf_op jit(solution)/shard_map/ppermute | solution.py:21
  457.6 2.9 collective-permute-done.59
  461.3 62.2 %psum.42 = f32[]{:T(128)} all-reduce(f32[]{:T(128)} %get-tuple-element.1161), channel_id=1, replica_groups=mesh['sky'=16,'depth'=8] {'sky','depth'}, use_global_device_ids=true, to_apply=%region_37.38 | all-reduce | flops 1 | bytes 8 | tf_op jit(solution)/shard_map/psum | solution.py:220
  (353 shorter events, 111.3 us)
Async XLA Ops:
  14.3 23.4 %collective-permute-start = (s32[3]{0:T(128)S(1)}, s32[3]{0:T(128)S(1)}, u32[]{:S(2)}, u32[]{:S(2)}) collective-permute-start(s32[3]{0:T(128)S(1)} %get-tuple-element.1142), channel_id=1, source_target_pairs={{0,8},{8,16},{16,24},{24,32},{32,40},{40,48},{48,56},{56,64},{64,7... | collective-permute-start | bytes 44 | tf_op jit(solution)/shard_map/ppermute | solution.py:15
  16.7 22.9 %collective-permute-start.2 = (s32[3]{0:T(128)S(1)}, s32[3]{0:T(128)S(1)}, u32[]{:S(2)}, u32[]{:S(2)}) collective-permute-start(s32[3]{0:T(128)S(1)} %get-tuple-element.1141), channel_id=1, source_target_pairs={{0,8},{8,16},{16,24},{24,32},{32,40},{40,48},{48,56},{56,64},{64,7... | collective-permute-start | bytes 44 | tf_op jit(solution)/shard_map/ppermute | solution.py:15
  18.4 26.1 %collective-permute-start.3 = (s32[3]{0:T(128)S(1)}, s32[3]{0:T(128)S(1)}, u32[]{:S(2)}, u32[]{:S(2)}) collective-permute-start(s32[3]{0:T(128)S(1)} %get-tuple-element.1140), channel_id=1, source_target_pairs={{0,8},{8,16},{16,24},{24,32},{32,40},{40,48},{48,56},{56,64},{64,7... | collective-permute-start | bytes 44 | tf_op jit(solution)/shard_map/ppermute | solution.py:15
  19.7 24.9 %collective-permute-start.5 = (s32[3]{0:T(128)S(1)}, s32[3]{0:T(128)S(1)}, u32[]{:S(2)}, u32[]{:S(2)}) collective-permute-start(s32[3]{0:T(128)S(1)} %get-tuple-element.1139), channel_id=1, source_target_pairs={{0,1},{1,2},{2,3},{3,4},{4,5},{5,6},{6,7},{8,9},{9,10},{10,11},{11... | collective-permute-start | bytes 44 | tf_op jit(solution)/shard_map/ppermute | solution.py:21
  26.4 44.1 %collective-permute-start.12 = (f32[3,3,128]{2,1,0:T(4,128)S(1)}, f32[3,3,128]{2,1,0:T(4,128)S(1)}, u32[]{:S(2)}, u32[]{:S(2)}) collective-permute-start(f32[3,3,128]{2,1,0:T(4,128)S(1)} %get-tuple-element.1133), channel_id=1, source_target_pairs={{0,8},{8,16},{16,24},{24,32},{32,40},{40,48},{48,56},{56,64},{64,7... | collective-permute-start | bytes 13832 | tf_op jit(solution)/shard_map/ppermute | solution.py:15
  37.7 7.0 %collective-permute-start.6 = (s32[3]{0:T(128)S(1)}, s32[3]{0:T(128)S(1)}, u32[]{:S(2)}, u32[]{:S(2)}) collective-permute-start(s32[3]{0:T(128)S(1)} %get-tuple-element.1138), channel_id=1, source_target_pairs={{1,0},{2,1},{3,2},{4,3},{5,4},{6,5},{7,6},{9,8},{10,9},{11,10},{12... | collective-permute-start | bytes 44 | tf_op jit(solution)/shard_map/ppermute | solution.py:21
  39.6 6.4 %collective-permute-start.7 = (s32[3]{0:T(128)S(1)}, s32[3]{0:T(128)S(1)}, u32[]{:S(2)}, u32[]{:S(2)}) collective-permute-start(s32[3]{0:T(128)S(1)} %get-tuple-element.1137), channel_id=1, source_target_pairs={{0,120},{8,0},{16,8},{24,16},{32,24},{40,32},{48,40},{56,48},{64,5... | collective-permute-start | bytes 44 | tf_op jit(solution)/shard_map/ppermute | solution.py:15
  44.6 7.9 %collective-permute-start.10 = (s32[3]{0:T(128)S(1)}, s32[3]{0:T(128)S(1)}, u32[]{:S(2)}, u32[]{:S(2)}) collective-permute-start(s32[3]{0:T(128)S(1)} %get-tuple-element.1135), channel_id=1, source_target_pairs={{0,120},{8,0},{16,8},{24,16},{32,24},{40,32},{48,40},{56,48},{64,5... | collective-permute-start | bytes 44 | tf_op jit(solution)/shard_map/ppermute | solution.py:15
  44.7 33.7 %collective-permute-start.14 = (f32[3,3,128]{2,1,0:T(4,128)S(1)}, f32[3,3,128]{2,1,0:T(4,128)S(1)}, u32[]{:S(2)}, u32[]{:S(2)}) collective-permute-start(f32[3,3,128]{2,1,0:T(4,128)S(1)} %get-tuple-element.1132), channel_id=1, source_target_pairs={{0,8},{8,16},{16,24},{24,32},{32,40},{40,48},{48,56},{56,64},{64,7... | collective-permute-start | bytes 13832 | tf_op jit(solution)/shard_map/ppermute | solution.py:15
  46.1 33.1 %collective-permute-start.15 = (f32[3,3,128]{2,1,0:T(4,128)S(1)}, f32[3,3,128]{2,1,0:T(4,128)S(1)}, u32[]{:S(2)}, u32[]{:S(2)}) collective-permute-start(f32[3,3,128]{2,1,0:T(4,128)S(1)} %get-tuple-element.1131), channel_id=1, source_target_pairs={{0,8},{8,16},{16,24},{24,32},{32,40},{40,48},{48,56},{56,64},{64,7... | collective-permute-start | bytes 13832 | tf_op jit(solution)/shard_map/ppermute | solution.py:15
  47.4 44.3 %collective-permute-start.17 = (f32[3,3,128]{2,1,0:T(4,128)S(1)}, f32[3,3,128]{2,1,0:T(4,128)S(1)}, u32[]{:S(2)}, u32[]{:S(2)}) collective-permute-start(f32[3,3,128]{2,1,0:T(4,128)S(1)} %get-tuple-element.1130), channel_id=1, source_target_pairs={{0,1},{1,2},{2,3},{3,4},{4,5},{5,6},{6,7},{8,9},{9,10},{10,11},{11... | collective-permute-start | bytes 13832 | tf_op jit(solution)/shard_map/ppermute | solution.py:21
  68.5 23.3 %collective-permute-start.18 = (f32[3,3,128]{2,1,0:T(4,128)S(1)}, f32[3,3,128]{2,1,0:T(4,128)S(1)}, u32[]{:S(2)}, u32[]{:S(2)}) collective-permute-start(f32[3,3,128]{2,1,0:T(4,128)S(1)} %get-tuple-element.1129), channel_id=1, source_target_pairs={{1,0},{2,1},{3,2},{4,3},{5,4},{6,5},{7,6},{9,8},{10,9},{11,10},{12... | collective-permute-start | bytes 13832 | tf_op jit(solution)/shard_map/ppermute | solution.py:21
  74.9 6.2 %collective-permute-start.19 = (f32[3,3,128]{2,1,0:T(4,128)S(1)}, f32[3,3,128]{2,1,0:T(4,128)S(1)}, u32[]{:S(2)}, u32[]{:S(2)}) collective-permute-start(f32[3,3,128]{2,1,0:T(4,128)S(1)} %get-tuple-element.1128), channel_id=1, source_target_pairs={{0,120},{8,0},{16,8},{24,16},{32,24},{40,32},{48,40},{56,48},{64,5... | collective-permute-start | bytes 13832 | tf_op jit(solution)/shard_map/ppermute | solution.py:15
  78.4 5.8 %collective-permute-start.22 = (f32[3,3,128]{2,1,0:T(4,128)S(1)}, f32[3,3,128]{2,1,0:T(4,128)S(1)}, u32[]{:S(2)}, u32[]{:S(2)}) collective-permute-start(f32[3,3,128]{2,1,0:T(4,128)S(1)} %get-tuple-element.1127), channel_id=1, source_target_pairs={{0,120},{8,0},{16,8},{24,16},{32,24},{40,32},{48,40},{56,48},{64,5... | collective-permute-start | bytes 13832 | tf_op jit(solution)/shard_map/ppermute | solution.py:15
  79.2 10.6 %collective-permute-start.16 = (f32[3,3,128]{2,1,0:T(4,128)S(1)}, f32[3,3,128]{2,1,0:T(4,128)S(1)}, u32[]{:S(2)}, u32[]{:S(2)}) collective-permute-start(f32[3,3,128]{2,1,0:T(4,128)S(1)} %collective-permute-done.15), channel_id=1, source_target_pairs={{1,0},{2,1},{3,2},{4,3},{5,4},{6,5},{7,6},{9,8},{10,9},{11,10},{12... | collective-permute-start | bytes 13832 | tf_op jit(solution)/shard_map/ppermute | solution.py:21
  81.1 10.7 %collective-permute-start.21 = (f32[3,3,128]{2,1,0:T(4,128)S(1)}, f32[3,3,128]{2,1,0:T(4,128)S(1)}, u32[]{:S(2)}, u32[]{:S(2)}) collective-permute-start(f32[3,3,128]{2,1,0:T(4,128)S(1)} %get-tuple-element.1134), channel_id=1, source_target_pairs={{0,120},{8,0},{16,8},{24,16},{32,24},{40,32},{48,40},{56,48},{64,5... | collective-permute-start | bytes 13832 | tf_op jit(solution)/shard_map/ppermute | solution.py:15
  84.2 7.6 %collective-permute-start.20 = (f32[3,3,128]{2,1,0:T(4,128)S(1)}, f32[3,3,128]{2,1,0:T(4,128)S(1)}, u32[]{:S(2)}, u32[]{:S(2)}) collective-permute-start(f32[3,3,128]{2,1,0:T(4,128)S(1)} %collective-permute-done.19), channel_id=1, source_target_pairs={{0,1},{1,2},{2,3},{3,4},{4,5},{5,6},{6,7},{8,9},{9,10},{10,11},{11... | collective-permute-start | bytes 13832 | tf_op jit(solution)/shard_map/ppermute | solution.py:21
  189.7 9.6 %collective-permute-start.24 = (f32[3,3,128]{2,1,0:T(4,128)S(1)}, f32[3,3,128]{2,1,0:T(4,128)S(1)}, u32[]{:S(2)}, u32[]{:S(2)}) collective-permute-start(f32[3,3,128]{2,1,0:T(4,128)S(1)} %get-tuple-element.1125), channel_id=1, source_target_pairs={{0,8},{8,16},{16,24},{24,32},{32,40},{40,48},{48,56},{56,64},{64,7... | collective-permute-start | bytes 13832 | tf_op jit(solution)/shard_map/ppermute | solution.py:15
  192.2 15.6 %collective-permute-start.26 = (f32[3,3,128]{2,1,0:T(4,128)S(1)}, f32[3,3,128]{2,1,0:T(4,128)S(1)}, u32[]{:S(2)}, u32[]{:S(2)}) collective-permute-start(f32[3,3,128]{2,1,0:T(4,128)S(1)} %get-tuple-element.1124), channel_id=1, source_target_pairs={{0,8},{8,16},{16,24},{24,32},{32,40},{40,48},{48,56},{56,64},{64,7... | collective-permute-start | bytes 13832 | tf_op jit(solution)/shard_map/ppermute | solution.py:15
  192.6 15.6 %collective-permute-start.27 = (f32[3,3,128]{2,1,0:T(4,128)S(1)}, f32[3,3,128]{2,1,0:T(4,128)S(1)}, u32[]{:S(2)}, u32[]{:S(2)}) collective-permute-start(f32[3,3,128]{2,1,0:T(4,128)S(1)} %get-tuple-element.1123), channel_id=1, source_target_pairs={{0,8},{8,16},{16,24},{24,32},{32,40},{40,48},{48,56},{56,64},{64,7... | collective-permute-start | bytes 13832 | tf_op jit(solution)/shard_map/ppermute | solution.py:15
  194.3 26.9 %collective-permute-start.29 = (f32[3,3,128]{2,1,0:T(4,128)S(1)}, f32[3,3,128]{2,1,0:T(4,128)S(1)}, u32[]{:S(2)}, u32[]{:S(2)}) collective-permute-start(f32[3,3,128]{2,1,0:T(4,128)S(1)} %get-tuple-element.1122), channel_id=1, source_target_pairs={{0,1},{1,2},{2,3},{3,4},{4,5},{5,6},{6,7},{8,9},{9,10},{10,11},{11... | collective-permute-start | bytes 13832 | tf_op jit(solution)/shard_map/ppermute | solution.py:21
  197.4 23.8 %collective-permute-start.30 = (f32[3,3,128]{2,1,0:T(4,128)S(1)}, f32[3,3,128]{2,1,0:T(4,128)S(1)}, u32[]{:S(2)}, u32[]{:S(2)}) collective-permute-start(f32[3,3,128]{2,1,0:T(4,128)S(1)} %get-tuple-element.1121), channel_id=1, source_target_pairs={{1,0},{2,1},{3,2},{4,3},{5,4},{6,5},{7,6},{9,8},{10,9},{11,10},{12... | collective-permute-start | bytes 13832 | tf_op jit(solution)/shard_map/ppermute | solution.py:21
  203.8 6.4 %collective-permute-start.31 = (f32[3,3,128]{2,1,0:T(4,128)S(1)}, f32[3,3,128]{2,1,0:T(4,128)S(1)}, u32[]{:S(2)}, u32[]{:S(2)}) collective-permute-start(f32[3,3,128]{2,1,0:T(4,128)S(1)} %get-tuple-element.1120), channel_id=1, source_target_pairs={{0,120},{8,0},{16,8},{24,16},{32,24},{40,32},{48,40},{56,48},{64,5... | collective-permute-start | bytes 13832 | tf_op jit(solution)/shard_map/ppermute | solution.py:15
  207.8 6.1 %collective-permute-start.34 = (f32[3,3,128]{2,1,0:T(4,128)S(1)}, f32[3,3,128]{2,1,0:T(4,128)S(1)}, u32[]{:S(2)}, u32[]{:S(2)}) collective-permute-start(f32[3,3,128]{2,1,0:T(4,128)S(1)} %get-tuple-element.1119), channel_id=1, source_target_pairs={{0,120},{8,0},{16,8},{24,16},{32,24},{40,32},{48,40},{56,48},{64,5... | collective-permute-start | bytes 13832 | tf_op jit(solution)/shard_map/ppermute | solution.py:15
  208.2 11.0 %collective-permute-start.28 = (f32[3,3,128]{2,1,0:T(4,128)S(1)}, f32[3,3,128]{2,1,0:T(4,128)S(1)}, u32[]{:S(2)}, u32[]{:S(2)}) collective-permute-start(f32[3,3,128]{2,1,0:T(4,128)S(1)} %collective-permute-done.27), channel_id=1, source_target_pairs={{1,0},{2,1},{3,2},{4,3},{5,4},{6,5},{7,6},{9,8},{10,9},{11,10},{12... | collective-permute-start | bytes 13832 | tf_op jit(solution)/shard_map/ppermute | solution.py:21
  210.2 11.1 %collective-permute-start.33 = (f32[3,3,128]{2,1,0:T(4,128)S(1)}, f32[3,3,128]{2,1,0:T(4,128)S(1)}, u32[]{:S(2)}, u32[]{:S(2)}) collective-permute-start(f32[3,3,128]{2,1,0:T(4,128)S(1)} %get-tuple-element.1126), channel_id=1, source_target_pairs={{0,120},{8,0},{16,8},{24,16},{32,24},{40,32},{48,40},{56,48},{64,5... | collective-permute-start | bytes 13832 | tf_op jit(solution)/shard_map/ppermute | solution.py:15
  213.9 7.4 %collective-permute-start.32 = (f32[3,3,128]{2,1,0:T(4,128)S(1)}, f32[3,3,128]{2,1,0:T(4,128)S(1)}, u32[]{:S(2)}, u32[]{:S(2)}) collective-permute-start(f32[3,3,128]{2,1,0:T(4,128)S(1)} %collective-permute-done.31), channel_id=1, source_target_pairs={{0,1},{1,2},{2,3},{3,4},{4,5},{5,6},{6,7},{8,9},{9,10},{10,11},{11... | collective-permute-start | bytes 13832 | tf_op jit(solution)/shard_map/ppermute | solution.py:21
  290.2 6.1 %collective-permute-start.36 = (f32[3,3,128]{2,1,0:T(4,128)S(1)}, f32[3,3,128]{2,1,0:T(4,128)S(1)}, u32[]{:S(2)}, u32[]{:S(2)}) collective-permute-start(f32[3,3,128]{2,1,0:T(4,128)S(1)} %bitcast.335), channel_id=1, source_target_pairs={{0,8},{8,16},{16,24},{24,32},{32,40},{40,48},{48,56},{56,64},{64,7... | collective-permute-start | bytes 13832 | tf_op jit(solution)/shard_map/ppermute | solution.py:15
  296.3 14.7 %collective-permute-start.37 = (f32[3,3,128]{2,1,0:T(4,128)S(1)}, f32[3,3,128]{2,1,0:T(4,128)S(1)}, u32[]{:S(2)}, u32[]{:S(2)}) collective-permute-start(f32[3,3,128]{2,1,0:T(4,128)S(1)} %collective-permute-done.36), channel_id=1, source_target_pairs={{0,1},{1,2},{2,3},{3,4},{4,5},{5,6},{6,7},{8,9},{9,10},{10,11},{11... | collective-permute-start | bytes 13832 | tf_op jit(solution)/shard_map/ppermute | solution.py:21
  306.5 9.4 %collective-permute-start.38 = (f32[3,3,128]{2,1,0:T(4,128)S(1)}, f32[3,3,128]{2,1,0:T(4,128)S(1)}, u32[]{:S(2)}, u32[]{:S(2)}) collective-permute-start(f32[3,3,128]{2,1,0:T(4,128)S(1)} %bitcast.332), channel_id=1, source_target_pairs={{0,8},{8,16},{16,24},{24,32},{32,40},{40,48},{48,56},{56,64},{64,7... | collective-permute-start | bytes 13832 | tf_op jit(solution)/shard_map/ppermute | solution.py:15
  306.6 10.8 %collective-permute-start.39 = (f32[3,3,128]{2,1,0:T(4,128)S(1)}, f32[3,3,128]{2,1,0:T(4,128)S(1)}, u32[]{:S(2)}, u32[]{:S(2)}) collective-permute-start(f32[3,3,128]{2,1,0:T(4,128)S(1)} %bitcast.331), channel_id=1, source_target_pairs={{0,8},{8,16},{16,24},{24,32},{32,40},{40,48},{48,56},{56,64},{64,7... | collective-permute-start | bytes 13832 | tf_op jit(solution)/shard_map/ppermute | solution.py:15
  306.6 21.8 %collective-permute-start.41 = (f32[3,3,128]{2,1,0:T(4,128)S(1)}, f32[3,3,128]{2,1,0:T(4,128)S(1)}, u32[]{:S(2)}, u32[]{:S(2)}) collective-permute-start(f32[3,3,128]{2,1,0:T(4,128)S(1)} %bitcast.330), channel_id=1, source_target_pairs={{0,1},{1,2},{2,3},{3,4},{4,5},{5,6},{6,7},{8,9},{9,10},{10,11},{11... | collective-permute-start | bytes 13832 | tf_op jit(solution)/shard_map/ppermute | solution.py:21
  308.6 19.9 %collective-permute-start.42 = (f32[3,3,128]{2,1,0:T(4,128)S(1)}, f32[3,3,128]{2,1,0:T(4,128)S(1)}, u32[]{:S(2)}, u32[]{:S(2)}) collective-permute-start(f32[3,3,128]{2,1,0:T(4,128)S(1)} %bitcast.329), channel_id=1, source_target_pairs={{1,0},{2,1},{3,2},{4,3},{5,4},{6,5},{7,6},{9,8},{10,9},{11,10},{12... | collective-permute-start | bytes 13832 | tf_op jit(solution)/shard_map/ppermute | solution.py:21
  311.0 8.2 %collective-permute-start.43 = (f32[3,3,128]{2,1,0:T(4,128)S(1)}, f32[3,3,128]{2,1,0:T(4,128)S(1)}, u32[]{:S(2)}, u32[]{:S(2)}) collective-permute-start(f32[3,3,128]{2,1,0:T(4,128)S(1)} %bitcast.334), channel_id=1, source_target_pairs={{0,120},{8,0},{16,8},{24,16},{32,24},{40,32},{48,40},{56,48},{64,5... | collective-permute-start | bytes 13832 | tf_op jit(solution)/shard_map/ppermute | solution.py:15
  315.9 5.9 %collective-permute-start.46 = (f32[3,3,128]{2,1,0:T(4,128)S(1)}, f32[3,3,128]{2,1,0:T(4,128)S(1)}, u32[]{:S(2)}, u32[]{:S(2)}) collective-permute-start(f32[3,3,128]{2,1,0:T(4,128)S(1)} %bitcast.333), channel_id=1, source_target_pairs={{0,120},{8,0},{16,8},{24,16},{32,24},{40,32},{48,40},{56,48},{64,5... | collective-permute-start | bytes 13832 | tf_op jit(solution)/shard_map/ppermute | solution.py:15
  317.3 9.2 %collective-permute-start.40 = (f32[3,3,128]{2,1,0:T(4,128)S(1)}, f32[3,3,128]{2,1,0:T(4,128)S(1)}, u32[]{:S(2)}, u32[]{:S(2)}) collective-permute-start(f32[3,3,128]{2,1,0:T(4,128)S(1)} %collective-permute-done.39), channel_id=1, source_target_pairs={{1,0},{2,1},{3,2},{4,3},{5,4},{6,5},{7,6},{9,8},{10,9},{11,10},{12... | collective-permute-start | bytes 13832 | tf_op jit(solution)/shard_map/ppermute | solution.py:21
  319.3 9.3 %collective-permute-start.45 = (f32[3,3,128]{2,1,0:T(4,128)S(1)}, f32[3,3,128]{2,1,0:T(4,128)S(1)}, u32[]{:S(2)}, u32[]{:S(2)}) collective-permute-start(f32[3,3,128]{2,1,0:T(4,128)S(1)} %bitcast.328), channel_id=1, source_target_pairs={{0,120},{8,0},{16,8},{24,16},{32,24},{40,32},{48,40},{56,48},{64,5... | collective-permute-start | bytes 13832 | tf_op jit(solution)/shard_map/ppermute | solution.py:15
  321.8 6.7 %collective-permute-start.44 = (f32[3,3,128]{2,1,0:T(4,128)S(1)}, f32[3,3,128]{2,1,0:T(4,128)S(1)}, u32[]{:S(2)}, u32[]{:S(2)}) collective-permute-start(f32[3,3,128]{2,1,0:T(4,128)S(1)} %collective-permute-done.43), channel_id=1, source_target_pairs={{0,1},{1,2},{2,3},{3,4},{4,5},{5,6},{6,7},{8,9},{9,10},{10,11},{11... | collective-permute-start | bytes 13832 | tf_op jit(solution)/shard_map/ppermute | solution.py:21
  425.8 10.1 %collective-permute-start.48 = (f32[3,3,128]{2,1,0:T(4,128)S(1)}, f32[3,3,128]{2,1,0:T(4,128)S(1)}, u32[]{:S(2)}, u32[]{:S(2)}) collective-permute-start(f32[3,3,128]{2,1,0:T(4,128)S(1)} %get-tuple-element.1109), channel_id=1, source_target_pairs={{0,8},{8,16},{16,24},{24,32},{32,40},{40,48},{48,56},{56,64},{64,7... | collective-permute-start | bytes 13832 | tf_op jit(solution)/shard_map/ppermute | solution.py:15
  428.5 15.6 %collective-permute-start.50 = (f32[3,3,128]{2,1,0:T(4,128)S(1)}, f32[3,3,128]{2,1,0:T(4,128)S(1)}, u32[]{:S(2)}, u32[]{:S(2)}) collective-permute-start(f32[3,3,128]{2,1,0:T(4,128)S(1)} %get-tuple-element.1108), channel_id=1, source_target_pairs={{0,8},{8,16},{16,24},{24,32},{32,40},{40,48},{48,56},{56,64},{64,7... | collective-permute-start | bytes 13832 | tf_op jit(solution)/shard_map/ppermute | solution.py:15
  428.7 15.9 %collective-permute-start.51 = (f32[3,3,128]{2,1,0:T(4,128)S(1)}, f32[3,3,128]{2,1,0:T(4,128)S(1)}, u32[]{:S(2)}, u32[]{:S(2)}) collective-permute-start(f32[3,3,128]{2,1,0:T(4,128)S(1)} %get-tuple-element.1107), channel_id=1, source_target_pairs={{0,8},{8,16},{16,24},{24,32},{32,40},{40,48},{48,56},{56,64},{64,7... | collective-permute-start | bytes 13832 | tf_op jit(solution)/shard_map/ppermute | solution.py:15
  430.7 26.9 %collective-permute-start.53 = (f32[3,3,128]{2,1,0:T(4,128)S(1)}, f32[3,3,128]{2,1,0:T(4,128)S(1)}, u32[]{:S(2)}, u32[]{:S(2)}) collective-permute-start(f32[3,3,128]{2,1,0:T(4,128)S(1)} %get-tuple-element.1106), channel_id=1, source_target_pairs={{0,1},{1,2},{2,3},{3,4},{4,5},{5,6},{6,7},{8,9},{9,10},{10,11},{11... | collective-permute-start | bytes 13832 | tf_op jit(solution)/shard_map/ppermute | solution.py:21
  434.0 23.5 %collective-permute-start.54 = (f32[3,3,128]{2,1,0:T(4,128)S(1)}, f32[3,3,128]{2,1,0:T(4,128)S(1)}, u32[]{:S(2)}, u32[]{:S(2)}) collective-permute-start(f32[3,3,128]{2,1,0:T(4,128)S(1)} %get-tuple-element.1105), channel_id=1, source_target_pairs={{1,0},{2,1},{3,2},{4,3},{5,4},{6,5},{7,6},{9,8},{10,9},{11,10},{12... | collective-permute-start | bytes 13832 | tf_op jit(solution)/shard_map/ppermute | solution.py:21
  440.3 6.2 %collective-permute-start.55 = (f32[3,3,128]{2,1,0:T(4,128)S(1)}, f32[3,3,128]{2,1,0:T(4,128)S(1)}, u32[]{:S(2)}, u32[]{:S(2)}) collective-permute-start(f32[3,3,128]{2,1,0:T(4,128)S(1)} %get-tuple-element.1104), channel_id=1, source_target_pairs={{0,120},{8,0},{16,8},{24,16},{32,24},{40,32},{48,40},{56,48},{64,5... | collective-permute-start | bytes 13832 | tf_op jit(solution)/shard_map/ppermute | solution.py:15
  444.1 6.1 %collective-permute-start.58 = (f32[3,3,128]{2,1,0:T(4,128)S(1)}, f32[3,3,128]{2,1,0:T(4,128)S(1)}, u32[]{:S(2)}, u32[]{:S(2)}) collective-permute-start(f32[3,3,128]{2,1,0:T(4,128)S(1)} %get-tuple-element.1103), channel_id=1, source_target_pairs={{0,120},{8,0},{16,8},{24,16},{32,24},{40,32},{48,40},{56,48},{64,5... | collective-permute-start | bytes 13832 | tf_op jit(solution)/shard_map/ppermute | solution.py:15
  444.6 10.9 %collective-permute-start.52 = (f32[3,3,128]{2,1,0:T(4,128)S(1)}, f32[3,3,128]{2,1,0:T(4,128)S(1)}, u32[]{:S(2)}, u32[]{:S(2)}) collective-permute-start(f32[3,3,128]{2,1,0:T(4,128)S(1)} %collective-permute-done.51), channel_id=1, source_target_pairs={{1,0},{2,1},{3,2},{4,3},{5,4},{6,5},{7,6},{9,8},{10,9},{11,10},{12... | collective-permute-start | bytes 13832 | tf_op jit(solution)/shard_map/ppermute | solution.py:21
  446.6 11.0 %collective-permute-start.57 = (f32[3,3,128]{2,1,0:T(4,128)S(1)}, f32[3,3,128]{2,1,0:T(4,128)S(1)}, u32[]{:S(2)}, u32[]{:S(2)}) collective-permute-start(f32[3,3,128]{2,1,0:T(4,128)S(1)} %get-tuple-element.1110), channel_id=1, source_target_pairs={{0,120},{8,0},{16,8},{24,16},{32,24},{40,32},{48,40},{56,48},{64,5... | collective-permute-start | bytes 13832 | tf_op jit(solution)/shard_map/ppermute | solution.py:15
  450.2 7.3 %collective-permute-start.56 = (f32[3,3,128]{2,1,0:T(4,128)S(1)}, f32[3,3,128]{2,1,0:T(4,128)S(1)}, u32[]{:S(2)}, u32[]{:S(2)}) collective-permute-start(f32[3,3,128]{2,1,0:T(4,128)S(1)} %collective-permute-done.55), channel_id=1, source_target_pairs={{0,1},{1,2},{2,3},{3,4},{4,5},{5,6},{6,7},{8,9},{9,10},{10,11},{11... | collective-permute-start | bytes 13832 | tf_op jit(solution)/shard_map/ppermute | solution.py:21
  (18 other events, 262.1 us)
where the time goes:
time: 535 us; the launch traced here: 525 us
  blocking collectives  250 us (47%)
  starting transfers between devices  140 us (26%)
  other arithmetic  89.7 us (17%)
  waiting for transfers between devices  26.4 us (5%)
  local copies, waits for them, and re-layouts  12.1 us (2%)
    psum x2, blocking collectives, body(): counts = lax.psum(0.5 * self_total + ghost_total, ('sky', 'depth'))  125 us
    psum x2, blocking collectives, body(): lax.psum((jnp.sum(gradient * gradient), valid_local), ('sky', 'depth'))  124 us
    ppermute x30, starting transfers between devices, from_behind_2(): lax.ppermute(value, axis, [(source, source + steps) for source in range(i...  87.8 us
    ppermute x30, starting transfers between devices, from_behind(): lax.ppermute(array, axis, [(i, (i + by) % size) for i in range(size)])  52.4 us
    reduce_sum x8, other arithmetic, block_forces(): jnp.sum(bin_pull[:, None, None, None] * scaled * kernel, axis=0)  26.9 us
    reduce_sum x8, other arithmetic, block_counts(): return jnp.sum(weight[None] * kernel, axis=(1, 2, 3))  25.4 us
    ppermute x30, waiting for transfers between devices, from_behind_2(): lax.ppermute(value, axis, [(source, source + steps) for source in range(i...  21.5 us
  transfers between devices with their start and end apart: 60, of which 12 were waited for; matrix products, arithmetic and copies ran while one was open for 4% of the time, Pallas kernels for 0%

commit v1 on v0

--- a/solution.py
+++ b/solution.py
@@ -1,3 +1,4 @@
+import functools
 import jax
 import jax.numpy as jnp
 from jax import lax
@@ -8,6 +9,13 @@
 INV_WIDTH = 16.0
 STEP_SIZE = 0.01
 ROW_BLOCK = 8
+
+
+def prepare_widths(local_array, along_axis, peer_axis):
+    return jax.lax.psum(jax.lax.psum(local_array, axis_name=along_axis), axis_name=peer_axis)
+
+
+face_cut = functools.partial(prepare_widths, along_axis="depth", peer_axis="sky")
 
 
 def from_behind(array, axis, by):
@@ -198,7 +206,7 @@
         left_pos = coords[:, pair_cells]
         self_total = block_counts(coords, point_mask, coords, point_mask, zero_shift, centres)
         ghost_total = ghost_counts(left_pos, left_mask, ghost_pos, ghost_mask, shifts, centres)
-        counts = lax.psum(0.5 * self_total + ghost_total, ("sky", "depth"))
+        counts = face_cut(0.5 * self_total + ghost_total)
         mean_count = jnp.mean(counts)
         bin_pull = (jnp.log(1.0 + counts) - target_log) * mean_count / (1.0 + counts)
         self_grad, unused_right = block_forces(

time: 535 us -> 504 us (0.942)
  blocking collectives: 250 us -> 206 us
  starting transfers between devices: 140 us -> 152 us
    psum x2 -> x4, blocking collectives: 125 us -> 81.4 us  [the longest x2 59.9 us: prepare_widths(): jax.lax.psum(jax.lax.psum(local_array, axis_name=along_axis), axis_name=p...]
    ppermute x30, starting transfers between devices: 87.8 us -> 102 us  [from_behind_2(): lax.ppermute(value, axis, [(source, source + steps) for source in range(i...]
  transfers between devices with their start and end apart: 60 -> 60, of which waited for: 12 -> 12; matrix products, arithmetic and copies ran while one was open for 4% -> 5% of each run, Pallas kernels for 0% -> 0%
where the time goes in v1:
time: 504 us; the launch traced here: 494 us
  blocking collectives  206 us (41%)
  starting transfers between devices  152 us (30%)
  other arithmetic  89.9 us (18%)
  waiting for transfers between devices  26.5 us (5%)
  local copies, waits for them, and re-layouts  12.1 us (2%)
    psum x2, blocking collectives, body(): lax.psum((jnp.sum(gradient * gradient), valid_local), ('sky', 'depth'))  125 us
    ppermute x30, starting transfers between devices, from_behind_2(): lax.ppermute(value, axis, [(source, source + steps) for source in range(i...  102 us
    psum x2, blocking collectives, prepare_widths(): jax.lax.psum(jax.lax.psum(local_array, axis_name=along_axis), axis_name=p...  59.9 us
    ppermute x30, starting transfers between devices, from_behind(): lax.ppermute(array, axis, [(i, (i + by) % size) for i in range(size)])  49.6 us
    reduce_sum x8, other arithmetic, block_forces(): jnp.sum(bin_pull[:, None, None, None] * scaled * kernel, axis=0)  26.9 us
    reduce_sum x8, other arithmetic, block_counts(): return jnp.sum(weight[None] * kernel, axis=(1, 2, 3))  25.4 us
    ppermute x30, waiting for transfers between devices, from_behind_2(): lax.ppermute(value, axis, [(source, source + steps) for source in range(i...  21.5 us
    psum x2, blocking collectives, prepare_widths(): jax.lax.psum(local_array, axis_name=along_axis)  21.5 us
  transfers between devices with their start and end apart: 60, of which 12 were waited for; matrix products, arithmetic and copies ran while one was open for 5% of the time, Pallas kernels for 0%

profile of v1, /device:TPU:1, one launch (start us, length us, event | category | flops | bytes accessed | tf_op | source)
XLA Modules:
  0.0 494.3 jit_solution(8473176873060150616)
XLA Ops:
  3.0 10.7 %fusion.60 = s32[128,3]{1,0:T(8,128)S(1)} fusion(s32[1,128,3]{2,1,0:T(8,128)S(1)} %copy.87, s32[]{:T(128)} %bitcast.31, s32[]{:T(128)} %bitcast.32, s32[]{:T(128)} %bitcast.33, s32[]{:T(128)} %bitcast.34, s32[]{:T(128)} %bitcast.35, s32[]{:T(128)} %bitcast.37, s32[]{:T(128)} %bitcast.36, s32[]{:T(128)} %bitcast.14, s32[]{:T(128)} %bitcast.16, s32[]{:T(128)} %bitcast.18, ...), kind=kLoop, calls=%fused_computation.175 | loop fusion | flops 13440 | bytes 3648 | tf_op jit(solution)/shard_map/jit(_where)/select_n | solution.py:188
  19.8 4.6 collective-permute-start.5
  31.3 5.1 %fusion.36 = f32[16]{0:T(128)S(1)} fusion(f32[16,128,128]{2,1,0:T(8,128)S(1)} %get-tuple-element.1164, f32[16]{0:T(128)S(1)} %add_multiply_fusion.4, f32[16,128,128]{2,1,0:T(8,128)S(1)} %get-tuple-element.1163), kind=kLoop, calls=%fused_computation.104 | loop fusion | flops 25165808 | bytes 2097280 | tf_op jit(solution)/shard_map/reduce_sum | solution.py:45
  39.8 4.8 collective-permute-start.7
  47.5 5.0 %collective-permute-start.17 = (f32[3,3,128]{2,1,0:T(4,128)S(1)}, f32[3,3,128]{2,1,0:T(4,128)S(1)}, u32[]{:S(2)}, u32[]{:S(2)}) collective-permute-start(f32[3,3,128]{2,1,0:T(4,128)S(1)} %get-tuple-element.1130), channel_id=1, source_target_pairs={{0,1},{1,2},{2,3},{3,4},{4,5},{5,6},{6,7},{8,9},{9,10},{10,11},{11... | collective-permute-start | bytes 13832 | tf_op jit(solution)/shard_map/ppermute | solution.py:29
  57.7 2.9 collective-permute-done.4
  65.7 2.9 collective-permute-done.11
  70.6 3.6 collective-permute-start.13
  75.0 3.4 collective-permute-start.19
  81.3 3.0 collective-permute-start.21
  84.3 5.6 %collective-permute-start.20 = (f32[3,3,128]{2,1,0:T(4,128)S(1)}, f32[3,3,128]{2,1,0:T(4,128)S(1)}, u32[]{:S(2)}, u32[]{:S(2)}) collective-permute-start(f32[3,3,128]{2,1,0:T(4,128)S(1)} %collective-permute-done.19), channel_id=1, source_target_pairs={{0,1},{1,2},{2,3},{3,4},{4,5},{5,6},{6,7},{8,9},{9,10},{10,11},{11... | collective-permute-start | bytes 13832 | tf_op jit(solution)/shard_map/ppermute | solution.py:29
  92.0 2.9 collective-permute-done.23
  94.9 10.7 %while.70 = (s32[]{:T(128)}, f32[16]{0:T(128)S(1)}, f32[24,128]{1,0:T(8,128)S(1)}, f32[24,128]{1,0:T(8,128)S(1)}, f32[3,24,128]{2,1,0:T(8,128)S(1)}, /*index=5*/...) while((s32[]{:T(128)}, f32[16]{0:T(128)S(1)}, ...), condition=%wide.region_5.6_spmd.clone, body=%wide.region_2.5_spmd.clone.sunk | while | flops 14286903 | bytes 3244889 | solution.py:79
  99.5 2.5 fusion.98
  103.0 2.5 fusion.98
  105.6 10.8 %psum.52 = f32[16]{0:T(128)S(1)} all-reduce(f32[16]{0:T(128)S(1)} %multiply_add_fusion.2), channel_id=1, replica_groups=mesh['sky'=16,'depth'=8] {'depth'}, use_global_device_ids=true, to_apply=%region_6.7 | all-reduce | flops 16 | bytes 128 | tf_op jit(solution)/shard_map/psum | solution.py:15
  116.5 29.8 %psum.53 = f32[16]{0:T(128)S(1)} all-reduce(f32[16]{0:T(128)S(1)} %psum.52), channel_id=1, replica_groups=mesh['sky'=16,'depth'=8] {'sky'}, use_global_device_ids=true, to_apply=%region_7.8 | all-reduce | flops 16 | bytes 128 | tf_op jit(solution)/shard_map/psum | solution.py:15
  147.6 5.4 %fusion.37 = f32[16,128,128]{2,1,0:T(8,128)S(1)} fusion(f32[16]{0:T(128)S(1)} %get-tuple-element.1089, f32[16]{0:T(128)S(1)} %add_multiply_fusion.4, f32[16,128,128]{2,1,0:T(8,128)S(1)} %get-tuple-element.1163), kind=kLoop, calls=%fused_computation.105 | loop fusion | flops 29097984 | bytes 2097280 | tf_op jit(solution)/shard_map/reduce_sum | solution.py:52
  153.3 14.3 %while.68 = (s32[]{:T(128)}, f32[3,24,128]{2,1,0:T(8,128)S(1)}, f32[3,24,128]{2,1,0:T(8,128)S(1)}, f32[24,128]{1,0:T(8,128)S(1)}, f32[24,128]{1,0:T(8,128)S(1)},...) while((s32[]{:T(128)}, f32[3,24,128]{2,1,0:T(8,128)S(1)}, ...), condition=%wide.region_16.17_spmd.clone, body=%wide.region_11.0_spmd.clone.sunk | while | flops 18740276 | bytes 4916107 | solution.py:97
  154.1 2.7 fusion.94
  158.9 2.7 fusion.94
  163.7 2.7 fusion.94
  170.5 10.3 %collective-permute-start.29 = (f32[3,3,128]{2,1,0:T(4,128)S(1)}, f32[3,3,128]{2,1,0:T(4,128)S(1)}, u32[]{:S(2)}, u32[]{:S(2)}) collective-permute-start(f32[3,3,128]{2,1,0:T(4,128)S(1)} %get-tuple-element.1122), channel_id=1, source_target_pairs={{0,1},{1,2},{2,3},{3,4},{4,5},{5,6},{6,7},{8,9},{9,10},{10,11},{11... | collective-permute-start | bytes 13832 | tf_op jit(solution)/shard_map/ppermute | solution.py:29
  183.3 3.1 collective-permute-start.25
  187.1 5.0 %collective-permute-start.31 = (f32[3,3,128]{2,1,0:T(4,128)S(1)}, f32[3,3,128]{2,1,0:T(4,128)S(1)}, u32[]{:S(2)}, u32[]{:S(2)}) collective-permute-start(f32[3,3,128]{2,1,0:T(4,128)S(1)} %get-tuple-element.1120), channel_id=1, source_target_pairs={{0,120},{8,0},{16,8},{24,16},{32,24},{40,32},{48,40},{56,48},{64,5... | collective-permute-start | bytes 13832 | tf_op jit(solution)/shard_map/ppermute | solution.py:23
  198.1 5.5 %collective-permute-start.32 = (f32[3,3,128]{2,1,0:T(4,128)S(1)}, f32[3,3,128]{2,1,0:T(4,128)S(1)}, u32[]{:S(2)}, u32[]{:S(2)}) collective-permute-start(f32[3,3,128]{2,1,0:T(4,128)S(1)} %collective-permute-done.31), channel_id=1, source_target_pairs={{0,1},{1,2},{2,3},{3,4},{4,5},{5,6},{6,7},{8,9},{9,10},{10,11},{11... | collective-permute-start | bytes 13832 | tf_op jit(solution)/shard_map/ppermute | solution.py:29
  205.7 2.9 collective-permute-done.35
  209.4 62.8 %all-reduce = (f32[]{:T(128)}, f32[]{:T(128)}) all-reduce(f32[]{:T(128)} %get-tuple-element.1159, f32[]{:T(128)} %fusion.76), channel_id=1, replica_groups=mesh['sky'=16,'depth'=8] {'sky','depth'}, use_global_device_ids=true, to_apply=%region_18.19 | all-reduce | flops 2 | bytes 16 | tf_op jit(solution)/shard_map/psum | solution.py:228
  276.2 4.9 collective-permute-done.36
  281.1 4.5 collective-permute-start.37
  285.6 5.1 %fusion.42 = f32[16]{0:T(128)S(1)} fusion(f32[16,128,128]{2,1,0:T(8,128)S(1)} %add_sqrt_fusion.4, f32[16,128,128]{2,1,0:T(8,128)S(1)} %get-tuple-element.1164, f32[16]{0:T(128)S(1)} %add_multiply_fusion.4), kind=kLoop, calls=%fused_computation.110 | loop fusion | flops 25165808 | bytes 2097280 | tf_op jit(solution)/shard_map/reduce_sum | solution.py:45
  295.9 4.8 collective-permute-start.43
  306.6 4.7 collective-permute-start.44
  313.4 2.9 collective-permute-done.47
  316.4 10.7 %while.71 = (s32[]{:T(128)}, f32[16]{0:T(128)S(1)}, f32[24,128]{1,0:T(8,128)S(1)}, f32[24,128]{1,0:T(8,128)S(1)}, f32[3,24,128]{2,1,0:T(8,128)S(1)}, /*index=5*/...) while((s32[]{:T(128)}, f32[16]{0:T(128)S(1)}, ...), condition=%wide.region_26.27_spmd.clone, body=%wide.region_23.26_spmd.clone.sunk | while | flops 14286903 | bytes 3244889 | solution.py:79
  327.1 10.7 %psum.56 = f32[16]{0:T(128)S(1)} all-reduce(f32[16]{0:T(128)S(1)} %multiply_add_fusion.1), channel_id=1, replica_groups=mesh['sky'=16,'depth'=8] {'depth'}, use_global_device_ids=true, to_apply=%region_27.28 | all-reduce | flops 16 | bytes 128 | tf_op jit(solution)/shard_map/psum | solution.py:15
  337.7 30.1 %psum.57 = f32[16]{0:T(128)S(1)} all-reduce(f32[16]{0:T(128)S(1)} %psum.56), channel_id=1, replica_groups=mesh['sky'=16,'depth'=8] {'sky'}, use_global_device_ids=true, to_apply=%region_28.29 | all-reduce | flops 16 | bytes 128 | tf_op jit(solution)/shard_map/psum | solution.py:15
  369.1 5.4 %fusion.43 = f32[16,128,128]{2,1,0:T(8,128)S(1)} fusion(f32[16]{0:T(128)S(1)} %get-tuple-element.1087, f32[16,128,128]{2,1,0:T(8,128)S(1)} %add_sqrt_fusion.4, f32[16]{0:T(128)S(1)} %add_multiply_fusion.4), kind=kLoop, calls=%fused_computation.111 | loop fusion | flops 29097984 | bytes 2097280 | tf_op jit(solution)/shard_map/reduce_sum | solution.py:52
  374.9 14.3 %while.69 = (s32[]{:T(128)}, f32[3,24,128]{2,1,0:T(8,128)S(1)}, f32[3,24,128]{2,1,0:T(8,128)S(1)}, f32[24,128]{1,0:T(8,128)S(1)}, f32[24,128]{1,0:T(8,128)S(1)},...) while((s32[]{:T(128)}, f32[3,24,128]{2,1,0:T(8,128)S(1)}, ...), condition=%wide.region_37.38_spmd.clone, body=%wide.region_32.0_spmd.clone.sunk | while | flops 18740276 | bytes 4916107 | solution.py:97
  375.7 2.7 fusion.96
  380.5 2.7 fusion.96
  385.2 2.7 fusion.96
  391.6 10.3 %collective-permute-start.53 = (f32[3,3,128]{2,1,0:T(4,128)S(1)}, f32[3,3,128]{2,1,0:T(4,128)S(1)}, u32[]{:S(2)}, u32[]{:S(2)}) collective-permute-start(f32[3,3,128]{2,1,0:T(4,128)S(1)} %get-tuple-element.1106), channel_id=1, source_target_pairs={{0,1},{1,2},{2,3},{3,4},{4,5},{5,6},{6,7},{8,9},{9,10},{10,11},{11... | collective-permute-start | bytes 13832 | tf_op jit(solution)/shard_map/ppermute | solution.py:29
  404.4 3.1 collective-permute-start.49
  408.2 5.0 %collective-permute-start.55 = (f32[3,3,128]{2,1,0:T(4,128)S(1)}, f32[3,3,128]{2,1,0:T(4,128)S(1)}, u32[]{:S(2)}, u32[]{:S(2)}) collective-permute-start(f32[3,3,128]{2,1,0:T(4,128)S(1)} %get-tuple-element.1104), channel_id=1, source_target_pairs={{0,120},{8,0},{16,8},{24,16},{32,24},{40,32},{48,40},{56,48},{64,5... | collective-permute-start | bytes 13832 | tf_op jit(solution)/shard_map/ppermute | solution.py:23
  419.2 5.5 %collective-permute-start.56 = (f32[3,3,128]{2,1,0:T(4,128)S(1)}, f32[3,3,128]{2,1,0:T(4,128)S(1)}, u32[]{:S(2)}, u32[]{:S(2)}) collective-permute-start(f32[3,3,128]{2,1,0:T(4,128)S(1)} %collective-permute-done.55), channel_id=1, source_target_pairs={{0,1},{1,2},{2,3},{3,4},{4,5},{5,6},{6,7},{8,9},{9,10},{10,11},{11... | collective-permute-start | bytes 13832 | tf_op jit(solution)/shard_map/ppermute | solution.py:29
  426.7 2.9 collective-permute-done.59
  430.4 62.4 %psum.58 = f32[]{:T(128)} all-reduce(f32[]{:T(128)} %get-tuple-element.1161), channel_id=1, replica_groups=mesh['sky'=16,'depth'=8] {'sky','depth'}, use_global_device_ids=true, to_apply=%region_39.40 | all-reduce | flops 1 | bytes 8 | tf_op jit(solution)/shard_map/psum | solution.py:228
  (355 shorter events, 115.0 us)
Async XLA Ops:
  14.3 23.5 %collective-permute-start = (s32[3]{0:T(128)S(1)}, s32[3]{0:T(128)S(1)}, u32[]{:S(2)}, u32[]{:S(2)}) collective-permute-start(s32[3]{0:T(128)S(1)} %get-tuple-element.1142), channel_id=1, source_target_pairs={{0,8},{8,16},{16,24},{24,32},{32,40},{40,48},{48,56},{56,64},{64,7... | collective-permute-start | bytes 44 | tf_op jit(solution)/shard_map/ppermute | solution.py:23
  16.8 22.9 %collective-permute-start.2 = (s32[3]{0:T(128)S(1)}, s32[3]{0:T(128)S(1)}, u32[]{:S(2)}, u32[]{:S(2)}) collective-permute-start(s32[3]{0:T(128)S(1)} %get-tuple-element.1141), channel_id=1, source_target_pairs={{0,8},{8,16},{16,24},{24,32},{32,40},{40,48},{48,56},{56,64},{64,7... | collective-permute-start | bytes 44 | tf_op jit(solution)/shard_map/ppermute | solution.py:23
  18.5 26.1 %collective-permute-start.3 = (s32[3]{0:T(128)S(1)}, s32[3]{0:T(128)S(1)}, u32[]{:S(2)}, u32[]{:S(2)}) collective-permute-start(s32[3]{0:T(128)S(1)} %get-tuple-element.1140), channel_id=1, source_target_pairs={{0,8},{8,16},{16,24},{24,32},{32,40},{40,48},{48,56},{56,64},{64,7... | collective-permute-start | bytes 44 | tf_op jit(solution)/shard_map/ppermute | solution.py:23
  19.8 24.9 %collective-permute-start.5 = (s32[3]{0:T(128)S(1)}, s32[3]{0:T(128)S(1)}, u32[]{:S(2)}, u32[]{:S(2)}) collective-permute-start(s32[3]{0:T(128)S(1)} %get-tuple-element.1139), channel_id=1, source_target_pairs={{0,1},{1,2},{2,3},{3,4},{4,5},{5,6},{6,7},{8,9},{9,10},{10,11},{11... | collective-permute-start | bytes 44 | tf_op jit(solution)/shard_map/ppermute | solution.py:29
  26.5 44.2 %collective-permute-start.12 = (f32[3,3,128]{2,1,0:T(4,128)S(1)}, f32[3,3,128]{2,1,0:T(4,128)S(1)}, u32[]{:S(2)}, u32[]{:S(2)}) collective-permute-start(f32[3,3,128]{2,1,0:T(4,128)S(1)} %get-tuple-element.1133), channel_id=1, source_target_pairs={{0,8},{8,16},{16,24},{24,32},{32,40},{40,48},{48,56},{56,64},{64,7... | collective-permute-start | bytes 13832 | tf_op jit(solution)/shard_map/ppermute | solution.py:23
  37.8 7.0 %collective-permute-start.6 = (s32[3]{0:T(128)S(1)}, s32[3]{0:T(128)S(1)}, u32[]{:S(2)}, u32[]{:S(2)}) collective-permute-start(s32[3]{0:T(128)S(1)} %get-tuple-element.1138), channel_id=1, source_target_pairs={{1,0},{2,1},{3,2},{4,3},{5,4},{6,5},{7,6},{9,8},{10,9},{11,10},{12... | collective-permute-start | bytes 44 | tf_op jit(solution)/shard_map/ppermute | solution.py:29
  39.8 6.4 %collective-permute-start.7 = (s32[3]{0:T(128)S(1)}, s32[3]{0:T(128)S(1)}, u32[]{:S(2)}, u32[]{:S(2)}) collective-permute-start(s32[3]{0:T(128)S(1)} %get-tuple-element.1137), channel_id=1, source_target_pairs={{0,120},{8,0},{16,8},{24,16},{32,24},{40,32},{48,40},{56,48},{64,5... | collective-permute-start | bytes 44 | tf_op jit(solution)/shard_map/ppermute | solution.py:23
  44.7 7.9 %collective-permute-start.10 = (s32[3]{0:T(128)S(1)}, s32[3]{0:T(128)S(1)}, u32[]{:S(2)}, u32[]{:S(2)}) collective-permute-start(s32[3]{0:T(128)S(1)} %get-tuple-element.1135), channel_id=1, source_target_pairs={{0,120},{8,0},{16,8},{24,16},{32,24},{40,32},{48,40},{56,48},{64,5... | collective-permute-start | bytes 44 | tf_op jit(solution)/shard_map/ppermute | solution.py:23
  44.8 33.7 %collective-permute-start.14 = (f32[3,3,128]{2,1,0:T(4,128)S(1)}, f32[3,3,128]{2,1,0:T(4,128)S(1)}, u32[]{:S(2)}, u32[]{:S(2)}) collective-permute-start(f32[3,3,128]{2,1,0:T(4,128)S(1)} %get-tuple-element.1132), channel_id=1, source_target_pairs={{0,8},{8,16},{16,24},{24,32},{32,40},{40,48},{48,56},{56,64},{64,7... | collective-permute-start | bytes 13832 | tf_op jit(solution)/shard_map/ppermute | solution.py:23
  46.2 33.1 %collective-permute-start.15 = (f32[3,3,128]{2,1,0:T(4,128)S(1)}, f32[3,3,128]{2,1,0:T(4,128)S(1)}, u32[]{:S(2)}, u32[]{:S(2)}) collective-permute-start(f32[3,3,128]{2,1,0:T(4,128)S(1)} %get-tuple-element.1131), channel_id=1, source_target_pairs={{0,8},{8,16},{16,24},{24,32},{32,40},{40,48},{48,56},{56,64},{64,7... | collective-permute-start | bytes 13832 | tf_op jit(solution)/shard_map/ppermute | solution.py:23
  47.5 44.3 %collective-permute-start.17 = (f32[3,3,128]{2,1,0:T(4,128)S(1)}, f32[3,3,128]{2,1,0:T(4,128)S(1)}, u32[]{:S(2)}, u32[]{:S(2)}) collective-permute-start(f32[3,3,128]{2,1,0:T(4,128)S(1)} %get-tuple-element.1130), channel_id=1, source_target_pairs={{0,1},{1,2},{2,3},{3,4},{4,5},{5,6},{6,7},{8,9},{9,10},{10,11},{11... | collective-permute-start | bytes 13832 | tf_op jit(solution)/shard_map/ppermute | solution.py:29
  68.6 23.3 %collective-permute-start.18 = (f32[3,3,128]{2,1,0:T(4,128)S(1)}, f32[3,3,128]{2,1,0:T(4,128)S(1)}, u32[]{:S(2)}, u32[]{:S(2)}) collective-permute-start(f32[3,3,128]{2,1,0:T(4,128)S(1)} %get-tuple-element.1129), channel_id=1, source_target_pairs={{1,0},{2,1},{3,2},{4,3},{5,4},{6,5},{7,6},{9,8},{10,9},{11,10},{12... | collective-permute-start | bytes 13832 | tf_op jit(solution)/shard_map/ppermute | solution.py:29
  75.0 6.2 %collective-permute-start.19 = (f32[3,3,128]{2,1,0:T(4,128)S(1)}, f32[3,3,128]{2,1,0:T(4,128)S(1)}, u32[]{:S(2)}, u32[]{:S(2)}) collective-permute-start(f32[3,3,128]{2,1,0:T(4,128)S(1)} %get-tuple-element.1128), channel_id=1, source_target_pairs={{0,120},{8,0},{16,8},{24,16},{32,24},{40,32},{48,40},{56,48},{64,5... | collective-permute-start | bytes 13832 | tf_op jit(solution)/shard_map/ppermute | solution.py:23
  78.5 5.8 %collective-permute-start.22 = (f32[3,3,128]{2,1,0:T(4,128)S(1)}, f32[3,3,128]{2,1,0:T(4,128)S(1)}, u32[]{:S(2)}, u32[]{:S(2)}) collective-permute-start(f32[3,3,128]{2,1,0:T(4,128)S(1)} %get-tuple-element.1127), channel_id=1, source_target_pairs={{0,120},{8,0},{16,8},{24,16},{32,24},{40,32},{48,40},{56,48},{64,5... | collective-permute-start | bytes 13832 | tf_op jit(solution)/shard_map/ppermute | solution.py:23
  79.3 10.6 %collective-permute-start.16 = (f32[3,3,128]{2,1,0:T(4,128)S(1)}, f32[3,3,128]{2,1,0:T(4,128)S(1)}, u32[]{:S(2)}, u32[]{:S(2)}) collective-permute-start(f32[3,3,128]{2,1,0:T(4,128)S(1)} %collective-permute-done.15), channel_id=1, source_target_pairs={{1,0},{2,1},{3,2},{4,3},{5,4},{6,5},{7,6},{9,8},{10,9},{11,10},{12... | collective-permute-start | bytes 13832 | tf_op jit(solution)/shard_map/ppermute | solution.py:29
  81.3 10.7 %collective-permute-start.21 = (f32[3,3,128]{2,1,0:T(4,128)S(1)}, f32[3,3,128]{2,1,0:T(4,128)S(1)}, u32[]{:S(2)}, u32[]{:S(2)}) collective-permute-start(f32[3,3,128]{2,1,0:T(4,128)S(1)} %get-tuple-element.1134), channel_id=1, source_target_pairs={{0,120},{8,0},{16,8},{24,16},{32,24},{40,32},{48,40},{56,48},{64,5... | collective-permute-start | bytes 13832 | tf_op jit(solution)/shard_map/ppermute | solution.py:23
  84.3 7.6 %collective-permute-start.20 = (f32[3,3,128]{2,1,0:T(4,128)S(1)}, f32[3,3,128]{2,1,0:T(4,128)S(1)}, u32[]{:S(2)}, u32[]{:S(2)}) collective-permute-start(f32[3,3,128]{2,1,0:T(4,128)S(1)} %collective-permute-done.19), channel_id=1, source_target_pairs={{0,1},{1,2},{2,3},{3,4},{4,5},{5,6},{6,7},{8,9},{9,10},{10,11},{11... | collective-permute-start | bytes 13832 | tf_op jit(solution)/shard_map/ppermute | solution.py:29
  167.7 15.6 %collective-permute-start.24 = (f32[3,3,128]{2,1,0:T(4,128)S(1)}, f32[3,3,128]{2,1,0:T(4,128)S(1)}, u32[]{:S(2)}, u32[]{:S(2)}) collective-permute-start(f32[3,3,128]{2,1,0:T(4,128)S(1)} %get-tuple-element.1125), channel_id=1, source_target_pairs={{0,8},{8,16},{16,24},{24,32},{32,40},{40,48},{48,56},{56,64},{64,7... | collective-permute-start | bytes 13832 | tf_op jit(solution)/shard_map/ppermute | solution.py:23
  170.3 21.9 %collective-permute-start.26 = (f32[3,3,128]{2,1,0:T(4,128)S(1)}, f32[3,3,128]{2,1,0:T(4,128)S(1)}, u32[]{:S(2)}, u32[]{:S(2)}) collective-permute-start(f32[3,3,128]{2,1,0:T(4,128)S(1)} %get-tuple-element.1124), channel_id=1, source_target_pairs={{0,8},{8,16},{16,24},{24,32},{32,40},{40,48},{48,56},{56,64},{64,7... | collective-permute-start | bytes 13832 | tf_op jit(solution)/shard_map/ppermute | solution.py:23
  170.4 23.5 %collective-permute-start.27 = (f32[3,3,128]{2,1,0:T(4,128)S(1)}, f32[3,3,128]{2,1,0:T(4,128)S(1)}, u32[]{:S(2)}, u32[]{:S(2)}) collective-permute-start(f32[3,3,128]{2,1,0:T(4,128)S(1)} %get-tuple-element.1123), channel_id=1, source_target_pairs={{0,8},{8,16},{16,24},{24,32},{32,40},{40,48},{48,56},{56,64},{64,7... | collective-permute-start | bytes 13832 | tf_op jit(solution)/shard_map/ppermute | solution.py:23
  170.5 35.1 %collective-permute-start.29 = (f32[3,3,128]{2,1,0:T(4,128)S(1)}, f32[3,3,128]{2,1,0:T(4,128)S(1)}, u32[]{:S(2)}, u32[]{:S(2)}) collective-permute-start(f32[3,3,128]{2,1,0:T(4,128)S(1)} %get-tuple-element.1122), channel_id=1, source_target_pairs={{0,1},{1,2},{2,3},{3,4},{4,5},{5,6},{6,7},{8,9},{9,10},{10,11},{11... | collective-permute-start | bytes 13832 | tf_op jit(solution)/shard_map/ppermute | solution.py:29
  180.8 24.8 %collective-permute-start.30 = (f32[3,3,128]{2,1,0:T(4,128)S(1)}, f32[3,3,128]{2,1,0:T(4,128)S(1)}, u32[]{:S(2)}, u32[]{:S(2)}) collective-permute-start(f32[3,3,128]{2,1,0:T(4,128)S(1)} %get-tuple-element.1121), channel_id=1, source_target_pairs={{1,0},{2,1},{3,2},{4,3},{5,4},{6,5},{7,6},{9,8},{10,9},{11,10},{12... | collective-permute-start | bytes 13832 | tf_op jit(solution)/shard_map/ppermute | solution.py:29
  187.1 8.6 %collective-permute-start.31 = (f32[3,3,128]{2,1,0:T(4,128)S(1)}, f32[3,3,128]{2,1,0:T(4,128)S(1)}, u32[]{:S(2)}, u32[]{:S(2)}) collective-permute-start(f32[3,3,128]{2,1,0:T(4,128)S(1)} %get-tuple-element.1120), channel_id=1, source_target_pairs={{0,120},{8,0},{16,8},{24,16},{32,24},{40,32},{48,40},{56,48},{64,5... | collective-permute-start | bytes 13832 | tf_op jit(solution)/shard_map/ppermute | solution.py:23
  192.2 5.9 %collective-permute-start.34 = (f32[3,3,128]{2,1,0:T(4,128)S(1)}, f32[3,3,128]{2,1,0:T(4,128)S(1)}, u32[]{:S(2)}, u32[]{:S(2)}) collective-permute-start(f32[3,3,128]{2,1,0:T(4,128)S(1)} %get-tuple-element.1119), channel_id=1, source_target_pairs={{0,120},{8,0},{16,8},{24,16},{32,24},{40,32},{48,40},{56,48},{64,5... | collective-permute-start | bytes 13832 | tf_op jit(solution)/shard_map/ppermute | solution.py:23
  193.9 9.7 %collective-permute-start.28 = (f32[3,3,128]{2,1,0:T(4,128)S(1)}, f32[3,3,128]{2,1,0:T(4,128)S(1)}, u32[]{:S(2)}, u32[]{:S(2)}) collective-permute-start(f32[3,3,128]{2,1,0:T(4,128)S(1)} %collective-permute-done.27), channel_id=1, source_target_pairs={{1,0},{2,1},{3,2},{4,3},{5,4},{6,5},{7,6},{9,8},{10,9},{11,10},{12... | collective-permute-start | bytes 13832 | tf_op jit(solution)/shard_map/ppermute | solution.py:29
  195.8 9.8 %collective-permute-start.33 = (f32[3,3,128]{2,1,0:T(4,128)S(1)}, f32[3,3,128]{2,1,0:T(4,128)S(1)}, u32[]{:S(2)}, u32[]{:S(2)}) collective-permute-start(f32[3,3,128]{2,1,0:T(4,128)S(1)} %get-tuple-element.1126), channel_id=1, source_target_pairs={{0,120},{8,0},{16,8},{24,16},{32,24},{40,32},{48,40},{56,48},{64,5... | collective-permute-start | bytes 13832 | tf_op jit(solution)/shard_map/ppermute | solution.py:23
  198.1 7.5 %collective-permute-start.32 = (f32[3,3,128]{2,1,0:T(4,128)S(1)}, f32[3,3,128]{2,1,0:T(4,128)S(1)}, u32[]{:S(2)}, u32[]{:S(2)}) collective-permute-start(f32[3,3,128]{2,1,0:T(4,128)S(1)} %collective-permute-done.31), channel_id=1, source_target_pairs={{0,1},{1,2},{2,3},{3,4},{4,5},{5,6},{6,7},{8,9},{9,10},{10,11},{11... | collective-permute-start | bytes 13832 | tf_op jit(solution)/shard_map/ppermute | solution.py:29
  275.2 5.9 %collective-permute-start.36 = (f32[3,3,128]{2,1,0:T(4,128)S(1)}, f32[3,3,128]{2,1,0:T(4,128)S(1)}, u32[]{:S(2)}, u32[]{:S(2)}) collective-permute-start(f32[3,3,128]{2,1,0:T(4,128)S(1)} %bitcast.335), channel_id=1, source_target_pairs={{0,8},{8,16},{16,24},{24,32},{32,40},{40,48},{48,56},{56,64},{64,7... | collective-permute-start | bytes 13832 | tf_op jit(solution)/shard_map/ppermute | solution.py:23
  281.1 14.8 %collective-permute-start.37 = (f32[3,3,128]{2,1,0:T(4,128)S(1)}, f32[3,3,128]{2,1,0:T(4,128)S(1)}, u32[]{:S(2)}, u32[]{:S(2)}) collective-permute-start(f32[3,3,128]{2,1,0:T(4,128)S(1)} %collective-permute-done.36), channel_id=1, source_target_pairs={{0,1},{1,2},{2,3},{3,4},{4,5},{5,6},{6,7},{8,9},{9,10},{10,11},{11... | collective-permute-start | bytes 13832 | tf_op jit(solution)/shard_map/ppermute | solution.py:29
  291.3 9.4 %collective-permute-start.38 = (f32[3,3,128]{2,1,0:T(4,128)S(1)}, f32[3,3,128]{2,1,0:T(4,128)S(1)}, u32[]{:S(2)}, u32[]{:S(2)}) collective-permute-start(f32[3,3,128]{2,1,0:T(4,128)S(1)} %bitcast.332), channel_id=1, source_target_pairs={{0,8},{8,16},{16,24},{24,32},{32,40},{40,48},{48,56},{56,64},{64,7... | collective-permute-start | bytes 13832 | tf_op jit(solution)/shard_map/ppermute | solution.py:23
  291.4 10.8 %collective-permute-start.39 = (f32[3,3,128]{2,1,0:T(4,128)S(1)}, f32[3,3,128]{2,1,0:T(4,128)S(1)}, u32[]{:S(2)}, u32[]{:S(2)}) collective-permute-start(f32[3,3,128]{2,1,0:T(4,128)S(1)} %bitcast.331), channel_id=1, source_target_pairs={{0,8},{8,16},{16,24},{24,32},{32,40},{40,48},{48,56},{56,64},{64,7... | collective-permute-start | bytes 13832 | tf_op jit(solution)/shard_map/ppermute | solution.py:23
  291.5 21.8 %collective-permute-start.41 = (f32[3,3,128]{2,1,0:T(4,128)S(1)}, f32[3,3,128]{2,1,0:T(4,128)S(1)}, u32[]{:S(2)}, u32[]{:S(2)}) collective-permute-start(f32[3,3,128]{2,1,0:T(4,128)S(1)} %bitcast.330), channel_id=1, source_target_pairs={{0,1},{1,2},{2,3},{3,4},{4,5},{5,6},{6,7},{8,9},{9,10},{10,11},{11... | collective-permute-start | bytes 13832 | tf_op jit(solution)/shard_map/ppermute | solution.py:29
  293.4 19.9 %collective-permute-start.42 = (f32[3,3,128]{2,1,0:T(4,128)S(1)}, f32[3,3,128]{2,1,0:T(4,128)S(1)}, u32[]{:S(2)}, u32[]{:S(2)}) collective-permute-start(f32[3,3,128]{2,1,0:T(4,128)S(1)} %bitcast.329), channel_id=1, source_target_pairs={{1,0},{2,1},{3,2},{4,3},{5,4},{6,5},{7,6},{9,8},{10,9},{11,10},{12... | collective-permute-start | bytes 13832 | tf_op jit(solution)/shard_map/ppermute | solution.py:29
  295.9 8.2 %collective-permute-start.43 = (f32[3,3,128]{2,1,0:T(4,128)S(1)}, f32[3,3,128]{2,1,0:T(4,128)S(1)}, u32[]{:S(2)}, u32[]{:S(2)}) collective-permute-start(f32[3,3,128]{2,1,0:T(4,128)S(1)} %bitcast.334), channel_id=1, source_target_pairs={{0,120},{8,0},{16,8},{24,16},{32,24},{40,32},{48,40},{56,48},{64,5... | collective-permute-start | bytes 13832 | tf_op jit(solution)/shard_map/ppermute | solution.py:23
  300.7 5.9 %collective-permute-start.46 = (f32[3,3,128]{2,1,0:T(4,128)S(1)}, f32[3,3,128]{2,1,0:T(4,128)S(1)}, u32[]{:S(2)}, u32[]{:S(2)}) collective-permute-start(f32[3,3,128]{2,1,0:T(4,128)S(1)} %bitcast.333), channel_id=1, source_target_pairs={{0,120},{8,0},{16,8},{24,16},{32,24},{40,32},{48,40},{56,48},{64,5... | collective-permute-start | bytes 13832 | tf_op jit(solution)/shard_map/ppermute | solution.py:23
  302.2 9.2 %collective-permute-start.40 = (f32[3,3,128]{2,1,0:T(4,128)S(1)}, f32[3,3,128]{2,1,0:T(4,128)S(1)}, u32[]{:S(2)}, u32[]{:S(2)}) collective-permute-start(f32[3,3,128]{2,1,0:T(4,128)S(1)} %collective-permute-done.39), channel_id=1, source_target_pairs={{1,0},{2,1},{3,2},{4,3},{5,4},{6,5},{7,6},{9,8},{10,9},{11,10},{12... | collective-permute-start | bytes 13832 | tf_op jit(solution)/shard_map/ppermute | solution.py:29
  304.1 9.3 %collective-permute-start.45 = (f32[3,3,128]{2,1,0:T(4,128)S(1)}, f32[3,3,128]{2,1,0:T(4,128)S(1)}, u32[]{:S(2)}, u32[]{:S(2)}) collective-permute-start(f32[3,3,128]{2,1,0:T(4,128)S(1)} %bitcast.328), channel_id=1, source_target_pairs={{0,120},{8,0},{16,8},{24,16},{32,24},{40,32},{48,40},{56,48},{64,5... | collective-permute-start | bytes 13832 | tf_op jit(solution)/shard_map/ppermute | solution.py:23
  306.6 6.7 %collective-permute-start.44 = (f32[3,3,128]{2,1,0:T(4,128)S(1)}, f32[3,3,128]{2,1,0:T(4,128)S(1)}, u32[]{:S(2)}, u32[]{:S(2)}) collective-permute-start(f32[3,3,128]{2,1,0:T(4,128)S(1)} %collective-permute-done.43), channel_id=1, source_target_pairs={{0,1},{1,2},{2,3},{3,4},{4,5},{5,6},{6,7},{8,9},{9,10},{10,11},{11... | collective-permute-start | bytes 13832 | tf_op jit(solution)/shard_map/ppermute | solution.py:29
  389.2 15.1 %collective-permute-start.48 = (f32[3,3,128]{2,1,0:T(4,128)S(1)}, f32[3,3,128]{2,1,0:T(4,128)S(1)}, u32[]{:S(2)}, u32[]{:S(2)}) collective-permute-start(f32[3,3,128]{2,1,0:T(4,128)S(1)} %get-tuple-element.1109), channel_id=1, source_target_pairs={{0,8},{8,16},{16,24},{24,32},{32,40},{40,48},{48,56},{56,64},{64,7... | collective-permute-start | bytes 13832 | tf_op jit(solution)/shard_map/ppermute | solution.py:23
  391.4 21.8 %collective-permute-start.50 = (f32[3,3,128]{2,1,0:T(4,128)S(1)}, f32[3,3,128]{2,1,0:T(4,128)S(1)}, u32[]{:S(2)}, u32[]{:S(2)}) collective-permute-start(f32[3,3,128]{2,1,0:T(4,128)S(1)} %get-tuple-element.1108), channel_id=1, source_target_pairs={{0,8},{8,16},{16,24},{24,32},{32,40},{40,48},{48,56},{56,64},{64,7... | collective-permute-start | bytes 13832 | tf_op jit(solution)/shard_map/ppermute | solution.py:23
  391.5 23.4 %collective-permute-start.51 = (f32[3,3,128]{2,1,0:T(4,128)S(1)}, f32[3,3,128]{2,1,0:T(4,128)S(1)}, u32[]{:S(2)}, u32[]{:S(2)}) collective-permute-start(f32[3,3,128]{2,1,0:T(4,128)S(1)} %get-tuple-element.1107), channel_id=1, source_target_pairs={{0,8},{8,16},{16,24},{24,32},{32,40},{40,48},{48,56},{56,64},{64,7... | collective-permute-start | bytes 13832 | tf_op jit(solution)/shard_map/ppermute | solution.py:23
  391.6 35.0 %collective-permute-start.53 = (f32[3,3,128]{2,1,0:T(4,128)S(1)}, f32[3,3,128]{2,1,0:T(4,128)S(1)}, u32[]{:S(2)}, u32[]{:S(2)}) collective-permute-start(f32[3,3,128]{2,1,0:T(4,128)S(1)} %get-tuple-element.1106), channel_id=1, source_target_pairs={{0,1},{1,2},{2,3},{3,4},{4,5},{5,6},{6,7},{8,9},{9,10},{10,11},{11... | collective-permute-start | bytes 13832 | tf_op jit(solution)/shard_map/ppermute | solution.py:29
  401.9 24.8 %collective-permute-start.54 = (f32[3,3,128]{2,1,0:T(4,128)S(1)}, f32[3,3,128]{2,1,0:T(4,128)S(1)}, u32[]{:S(2)}, u32[]{:S(2)}) collective-permute-start(f32[3,3,128]{2,1,0:T(4,128)S(1)} %get-tuple-element.1105), channel_id=1, source_target_pairs={{1,0},{2,1},{3,2},{4,3},{5,4},{6,5},{7,6},{9,8},{10,9},{11,10},{12... | collective-permute-start | bytes 13832 | tf_op jit(solution)/shard_map/ppermute | solution.py:29
  408.2 8.6 %collective-permute-start.55 = (f32[3,3,128]{2,1,0:T(4,128)S(1)}, f32[3,3,128]{2,1,0:T(4,128)S(1)}, u32[]{:S(2)}, u32[]{:S(2)}) collective-permute-start(f32[3,3,128]{2,1,0:T(4,128)S(1)} %get-tuple-element.1104), channel_id=1, source_target_pairs={{0,120},{8,0},{16,8},{24,16},{32,24},{40,32},{48,40},{56,48},{64,5... | collective-permute-start | bytes 13832 | tf_op jit(solution)/shard_map/ppermute | solution.py:23
  413.3 5.9 %collective-permute-start.58 = (f32[3,3,128]{2,1,0:T(4,128)S(1)}, f32[3,3,128]{2,1,0:T(4,128)S(1)}, u32[]{:S(2)}, u32[]{:S(2)}) collective-permute-start(f32[3,3,128]{2,1,0:T(4,128)S(1)} %get-tuple-element.1103), channel_id=1, source_target_pairs={{0,120},{8,0},{16,8},{24,16},{32,24},{40,32},{48,40},{56,48},{64,5... | collective-permute-start | bytes 13832 | tf_op jit(solution)/shard_map/ppermute | solution.py:23
  414.9 9.7 %collective-permute-start.52 = (f32[3,3,128]{2,1,0:T(4,128)S(1)}, f32[3,3,128]{2,1,0:T(4,128)S(1)}, u32[]{:S(2)}, u32[]{:S(2)}) collective-permute-start(f32[3,3,128]{2,1,0:T(4,128)S(1)} %collective-permute-done.51), channel_id=1, source_target_pairs={{1,0},{2,1},{3,2},{4,3},{5,4},{6,5},{7,6},{9,8},{10,9},{11,10},{12... | collective-permute-start | bytes 13832 | tf_op jit(solution)/shard_map/ppermute | solution.py:29
  416.9 9.8 %collective-permute-start.57 = (f32[3,3,128]{2,1,0:T(4,128)S(1)}, f32[3,3,128]{2,1,0:T(4,128)S(1)}, u32[]{:S(2)}, u32[]{:S(2)}) collective-permute-start(f32[3,3,128]{2,1,0:T(4,128)S(1)} %get-tuple-element.1110), channel_id=1, source_target_pairs={{0,120},{8,0},{16,8},{24,16},{32,24},{40,32},{48,40},{56,48},{64,5... | collective-permute-start | bytes 13832 | tf_op jit(solution)/shard_map/ppermute | solution.py:23
  419.2 7.5 %collective-permute-start.56 = (f32[3,3,128]{2,1,0:T(4,128)S(1)}, f32[3,3,128]{2,1,0:T(4,128)S(1)}, u32[]{:S(2)}, u32[]{:S(2)}) collective-permute-start(f32[3,3,128]{2,1,0:T(4,128)S(1)} %collective-permute-done.55), channel_id=1, source_target_pairs={{0,1},{1,2},{2,3},{3,4},{4,5},{5,6},{6,7},{8,9},{9,10},{10,11},{11... | collective-permute-start | bytes 13832 | tf_op jit(solution)/shard_map/ppermute | solution.py:29
  (18 other events, 239.3 us)
